TPU v7x, 32 devices: a whole 2x2x4 slice. The times are simulated.
32 devices in a mesh: groups: 2 (over y), seq: 8 (over z, x), heads: 2 (over core).
Axes of the slice: x: 2, y: 2, z: 4, core: 2. Of those that a mesh axis runs over, the one named last changes fastest.
Arguments:
- queries: bfloat16 [2, 16, 16, 4096], P(None, ('groups', 'seq'), None, 'heads'), parts along dimension 1, may hold values from -8 to 8
- keys: bfloat16 [16, 4096, 512], P(('groups', 'seq'), None, 'heads'), parts along dimension 0, may hold values from -8 to 8
- values: bfloat16 [16, 4096, 512], P(('groups', 'seq'), None, 'heads'), parts along dimension 0, may hold values from -6 to 6
- tile_blocks: int32 [32, 4], P('groups'), parts along dimension 0, may hold values from 0 to 7, all different within a row; in each aligned block of 8 rows (0 to 7, 8 to 15, ...) at most 8 rows name the same one
- block_place: int32 [16], P('groups'), parts along dimension 0, may hold values from 0 to 7, each once
- tile_offset: int32 [32], P('groups'), parts along dimension 0, may hold values from 0 to 255
Outputs:
- attended: bfloat16 [2, 16, 16, 4096], P(None, ('groups', 'seq'), None, 'heads'), parts along dimension 1
There are 2 independent parts, one for each index of `groups`. A program takes and returns all parts, laid end to end along the dimension named above; each array names one. Nothing has to cross between parts.
Inputs may be any that keep to these rules, and one draw needn't show every extreme that they name: `tile_blocks`: each tile lists 4 different blocks; among the 8 tiles of one micro-batch no block is listed by more than 8 tiles, and in some micro-batch one block is listed by exactly 8. `block_place`: each index appears once.
All inputs are finite; a program needn't handle non-finite values.
Results may differ from a plain program's by a relative error of at most 0.0048.
Values may be sent and summed in bfloat16 or wider, within the bound.
A program may use at most 128 MiB of HBM per device.

v0:
```python
import jax
import jax.numpy as jnp
from jax import lax
from jax.sharding import PartitionSpec as P

HEAD = 128
BLOCK = 4096
TOP = 4


def attend(tile_query, key_head, value_head, horizon):
    scores = jnp.einsum(
        "rgh,kh->grk", tile_query, key_head, preferred_element_type=jnp.float32
    ) * HEAD ** (-0.5)
    visible = jnp.arange(key_head.shape[0], dtype=jnp.int32)[None, :] <= horizon[:, None]
    scores = jnp.where(visible[None], scores, -1e30)
    highest = jnp.max(scores, axis=2, keepdims=True)
    weights = jnp.exp(scores - highest)
    summed = jnp.sum(weights, axis=2, keepdims=True)
    blended = (
        jnp.einsum(
            "grk,kh->grh",
            weights.astype(jnp.bfloat16),
            value_head,
            preferred_element_type=jnp.float32,
        )
        / summed
    )
    return (blended, (highest + jnp.log(summed))[..., 0])


def local(queries, keys, values, tile_blocks, block_place, tile_offset):
    seq_size = lax.axis_size("seq")
    my_index = lax.axis_index("seq")
    batch_total = queries.shape[0]
    tile_rows = queries.shape[2]
    features = queries.shape[3]
    shared_heads = keys.shape[2] // HEAD
    group_size = features // keys.shape[2]
    head_count = shared_heads * group_size
    block_count = block_place.shape[0]
    key_heads = keys[0].reshape(BLOCK, shared_heads, HEAD).transpose(1, 0, 2)
    value_heads = values[0].reshape(BLOCK, shared_heads, HEAD).transpose(1, 0, 2)
    block_ids = jnp.arange(block_count, dtype=jnp.int32)
    my_block = jnp.sum(jnp.where(block_place == my_index, block_ids, 0))
    device_ids = jnp.arange(seq_size, dtype=jnp.int32)
    all_owners = jnp.sum(
        jnp.where(
            tile_blocks[:, :, None] == block_ids[None, None, :], block_place[None, None, :], 0
        ),
        axis=2,
    )
    halves = []
    for batch_id in range(batch_total):
        first_row = batch_id * seq_size
        local_query = queries[batch_id : batch_id + 1]
        block_lists = tile_blocks[first_row : first_row + seq_size]
        owners = all_owners[first_row : first_row + seq_size]
        batch_here = local_query.shape[0]
        tile_count = block_lists.shape[0]
        capacity = batch_here * min(seq_size, 3 * TOP)
        is_mine = jnp.any(owners == my_index, axis=1)
        listed = is_mine.astype(jnp.int32)
        ordinal = jnp.cumsum(listed) - listed
        chosen = is_mine[:, None] & (
            ordinal[:, None] == jnp.arange(capacity, dtype=jnp.int32)[None, :]
        )
        tile_ids = jnp.arange(tile_count, dtype=jnp.int32)
        slot_tile = jnp.sum(jnp.where(chosen, tile_ids[:, None], 0), axis=0)
        slot_live = jnp.any(chosen, axis=0)
        tile_owners = owners.reshape(batch_here, seq_size, TOP)
        my_owners = lax.dynamic_index_in_dim(tile_owners, my_index, axis=1, keepdims=False)
        send_to = jnp.any(my_owners[:, :, None] == device_ids[None, None, :], axis=1)
        outgoing = jnp.where(send_to[:, :, None, None], local_query, jnp.zeros((), jnp.bfloat16))
        gathered = lax.all_to_all(outgoing, "seq", split_axis=1, concat_axis=1, tiled=True)
        flat_tiles = gathered.reshape(tile_count, tile_rows, features)
        arrived = jnp.einsum(
            "hm,hnq->mnq",
            chosen.astype(jnp.bfloat16),
            flat_tiles,
            preferred_element_type=jnp.float32,
        ).astype(jnp.bfloat16)
        own_slot = jnp.max(block_lists[slot_tile], axis=1) == my_block
        row_ids = jnp.arange(tile_rows, dtype=jnp.int32)
        horizons = jnp.where(
            own_slot[:, None],
            tile_offset[first_row : first_row + seq_size][slot_tile][:, None] * tile_rows
            + row_ids[None, :],
            BLOCK,
        )

        def one_slot(bundle):
            tile_query, horizon, live = bundle
            split_query = tile_query.reshape(tile_rows, shared_heads, group_size, HEAD).transpose(
                1, 0, 2, 3
            )

            def compute(unused):
                blended, mass = lax.map(
                    lambda heads_bundle: attend(
                        heads_bundle[0], heads_bundle[1], heads_bundle[2], horizon
                    ),
                    (split_query, key_heads, value_heads),
                )
                return (
                    blended.transpose(2, 0, 1, 3).reshape(tile_rows, features),
                    mass.transpose(2, 0, 1).reshape(tile_rows, head_count),
                )

            def nothing(unused):
                return (
                    jnp.zeros((tile_rows, features), jnp.float32),
                    jnp.zeros((tile_rows, head_count), jnp.float32),
                )

            return lax.cond(live, compute, nothing, 0)

        partial_out, partial_mass = lax.map(one_slot, (arrived, horizons, slot_live))
        target = jnp.where(slot_live, slot_tile, tile_count)
        out_rows = (
            jnp.zeros((tile_count, tile_rows, features), jnp.float32)
            .at[target]
            .set(partial_out, mode="drop")
        )
        out_mass = (
            jnp.zeros((tile_count, tile_rows, head_count), jnp.float32)
            .at[target]
            .set(partial_mass, mode="drop")
        )
        returned = lax.all_to_all(
            out_rows.reshape(batch_here, seq_size, tile_rows, features),
            "seq",
            split_axis=1,
            concat_axis=1,
            tiled=True,
        )
        returned_mass = lax.all_to_all(
            out_mass.reshape(batch_here, seq_size, tile_rows, head_count),
            "seq",
            split_axis=1,
            concat_axis=1,
            tiled=True,
        )
        batch_ids = jnp.arange(batch_here, dtype=jnp.int32)[:, None]
        pieces = returned[batch_ids, my_owners]
        masses = returned_mass[batch_ids, my_owners]
        highest = jnp.max(masses, axis=1, keepdims=True)
        weight_share = jnp.exp(masses - highest)
        weight_share = weight_share / jnp.sum(weight_share, axis=1, keepdims=True)
        blended = jnp.sum(jnp.repeat(weight_share, HEAD, axis=3) * pieces, axis=1)
        halves.append(blended[:, None].astype(jnp.bfloat16))
    return jnp.concatenate(halves, axis=0)


def solution(mesh):
    placed = (
        P(None, ("groups", "seq"), None, "heads"),
        P(("groups", "seq"), None, "heads"),
        P(("groups", "seq"), None, "heads"),
        P("groups", None),
        P("groups"),
        P("groups"),
    )
    return jax.shard_map(
        local,
        mesh=mesh,
        in_specs=placed,
        out_specs=P(None, ("groups", "seq"), None, "heads"),
        check_vma=False,
    )
```

profile of v0, /device:TPU:0, one launch (start us, length us, event | category | flops | bytes accessed | tf_op | source)
XLA Modules:
  0.0 304.9 jit_solution(1879499270316512934)
XLA Ops:
  3.5 7.3 %all-to-all-start = ((bf16[1,8,16,2048]{3,2,0,1:T(8,128)(2,1)}), bf16[1,8,16,2048]{3,2,0,1:T(8,128)(2,1)S(1)}, u32[]{:S(2)}, u32[]{:S(2)}) async-start(bf16[1,8,16,2048]{3,2,0,1:T(8,128)(2,1)} %broadcast_select_fusion.1), calls=%async_computation | async-start | bytes 1048576 | tf_op jit(solution)/shard_map/all_to_all | solution.py:75
  25.7 4.1 %copy.88 = bf16[1,4096,256]{1,2,0:T(8,128)(2,1)} copy(bf16[1,4096,256]{2,1,0:T(8,128)(2,1)} %param.20) | data formatting | bytes 4194304 | tf_op args[2]
  29.8 3.1 %copy.93 = bf16[2,4096,128]{2,1,0:T(8,128)(2,1)S(1)} copy(bf16[2,4096,128]{1,2,0:T(8,128)(2,1)} %bitcast.241) | data formatting | bytes 4194304
  36.6 6.0 %all-to-all-start.3 = ((bf16[1,8,16,2048]{3,2,0,1:T(8,128)(2,1)}), bf16[1,8,16,2048]{3,2,0,1:T(8,128)(2,1)}, u32[]{:S(2)}, u32[]{:S(2)}) async-start(bf16[1,8,16,2048]{3,2,0,1:T(8,128)(2,1)} %broadcast_select_fusion), calls=%async_computation.3 | async-start | bytes 1048576 | tf_op jit(solution)/shard_map/all_to_all | solution.py:75
  44.2 59.8 %while.60 = (s32[]{:T(128)}, f32[8,16,2048]{2,1,0:T(8,128)S(1)}, f32[8,16,16]{2,1,0:T(8,128)S(1)}, pred[8]{0:T(512)(128)(4,1)}, bf16[8,16,2048]{2,1,0:T(8,128)(2...) while((s32[]{:T(128)}, f32[8,16,2048]{2,1,0:T(8,128)S(1)}, ...), condition=%wide.region_15.16_spmd.clone, body=%wide.region_8.15_spmd.clone.sunk | while | flops 272187520 | bytes 9769553 | solution.py:118
  47.0 7.2 %conditional.6 = (f32[1,16,2048]{2,1,0:T(8,128)S(1)}, f32[1,16,16]{1,2,0:T(8,128)}) conditional(s32[]{:T(128)} %bitcast.223, () %tuple.136, (pred[8]{0:T(512)(128)(4,1)S(1)}, s32[]{:T(128)}, bf16[2,4096,128]{2,1,0:T(8,128)(2,1)}, bf16[2,16,8,128]{3,2,0,1:T(8,128)(2,1)S(1)}, bf16[2,4096,128]{2,1,0:T(8,128)(2,1)S(1)}, ...), branch_computations={%region_9.9_spmd, %region_10.14_spmd.clone} | conditional | flops 272187520 | bytes 9226141 | solution.py:116
  47.1 6.9 %while.58 = (s32[]{:T(128)}, f32[2,8,16,128]{3,2,1,0:T(8,128)S(1)}, f32[2,8,16]{2,1,0:T(8,128)}, s32[16]{0:T(128)S(1)}, bf16[2,4096,128]{2,1,0:T(8,128)(2,1)}, /...) while((s32[]{:T(128)}, f32[2,8,16,128]{3,2,1,0:T(8,128)S(1)}, ...), condition=%wide.region_14.13_spmd, body=%wide.region_11.12_spmd.sunk | while | flops 272187264 | bytes 8700569 | solution.py:99
  57.7 7.2 %conditional.6 = (f32[1,16,2048]{2,1,0:T(8,128)S(1)}, f32[1,16,16]{1,2,0:T(8,128)}) conditional(s32[]{:T(128)} %bitcast.223, () %tuple.136, (pred[8]{0:T(512)(128)(4,1)S(1)}, s32[]{:T(128)}, bf16[2,4096,128]{2,1,0:T(8,128)(2,1)}, bf16[2,16,8,128]{3,2,0,1:T(8,128)(2,1)S(1)}, bf16[2,4096,128]{2,1,0:T(8,128)(2,1)S(1)}, ...), branch_computations={%region_9.9_spmd, %region_10.14_spmd.clone} | conditional | flops 272187520 | bytes 9226141 | solution.py:116
  57.9 6.9 %while.58 = (s32[]{:T(128)}, f32[2,8,16,128]{3,2,1,0:T(8,128)S(1)}, f32[2,8,16]{2,1,0:T(8,128)}, s32[16]{0:T(128)S(1)}, bf16[2,4096,128]{2,1,0:T(8,128)(2,1)}, /...) while((s32[]{:T(128)}, f32[2,8,16,128]{3,2,1,0:T(8,128)S(1)}, ...), condition=%wide.region_14.13_spmd, body=%wide.region_11.12_spmd.sunk | while | flops 272187264 | bytes 8700569 | solution.py:99
  68.5 7.2 %conditional.6 = (f32[1,16,2048]{2,1,0:T(8,128)S(1)}, f32[1,16,16]{1,2,0:T(8,128)}) conditional(s32[]{:T(128)} %bitcast.223, () %tuple.136, (pred[8]{0:T(512)(128)(4,1)S(1)}, s32[]{:T(128)}, bf16[2,4096,128]{2,1,0:T(8,128)(2,1)}, bf16[2,16,8,128]{3,2,0,1:T(8,128)(2,1)S(1)}, bf16[2,4096,128]{2,1,0:T(8,128)(2,1)S(1)}, ...), branch_computations={%region_9.9_spmd, %region_10.14_spmd.clone} | conditional | flops 272187520 | bytes 9226141 | solution.py:116
  68.6 6.9 %while.58 = (s32[]{:T(128)}, f32[2,8,16,128]{3,2,1,0:T(8,128)S(1)}, f32[2,8,16]{2,1,0:T(8,128)}, s32[16]{0:T(128)S(1)}, bf16[2,4096,128]{2,1,0:T(8,128)(2,1)}, /...) while((s32[]{:T(128)}, f32[2,8,16,128]{3,2,1,0:T(8,128)S(1)}, ...), condition=%wide.region_14.13_spmd, body=%wide.region_11.12_spmd.sunk | while | flops 272187264 | bytes 8700569 | solution.py:99
  79.2 7.2 %conditional.6 = (f32[1,16,2048]{2,1,0:T(8,128)S(1)}, f32[1,16,16]{1,2,0:T(8,128)}) conditional(s32[]{:T(128)} %bitcast.223, () %tuple.136, (pred[8]{0:T(512)(128)(4,1)S(1)}, s32[]{:T(128)}, bf16[2,4096,128]{2,1,0:T(8,128)(2,1)}, bf16[2,16,8,128]{3,2,0,1:T(8,128)(2,1)S(1)}, bf16[2,4096,128]{2,1,0:T(8,128)(2,1)S(1)}, ...), branch_computations={%region_9.9_spmd, %region_10.14_spmd.clone} | conditional | flops 272187520 | bytes 9226141 | solution.py:116
  79.3 6.9 %while.58 = (s32[]{:T(128)}, f32[2,8,16,128]{3,2,1,0:T(8,128)S(1)}, f32[2,8,16]{2,1,0:T(8,128)}, s32[16]{0:T(128)S(1)}, bf16[2,4096,128]{2,1,0:T(8,128)(2,1)}, /...) while((s32[]{:T(128)}, f32[2,8,16,128]{3,2,1,0:T(8,128)S(1)}, ...), condition=%wide.region_14.13_spmd, body=%wide.region_11.12_spmd.sunk | while | flops 272187264 | bytes 8700569 | solution.py:99
  105.6 29.4 %all-to-all-start.1 = ((f32[8,1,256]{2,1,0:T(1,128)}), f32[8,1,256]{2,1,0:T(1,128)S(1)}, u32[]{:S(2)}, u32[]{:S(2)}) async-start(f32[8,1,256]{2,1,0:T(1,128)} %reshape.624), calls=%async_computation.1 | async-start | bytes 16384 | tf_op jit(solution)/shard_map/all_to_all | solution.py:137
  138.7 53.1 %while.61 = (s32[]{:T(128)}, f32[8,16,2048]{2,1,0:T(8,128)}, f32[8,16,16]{2,1,0:T(8,128)S(1)}, pred[8]{0:T(512)(128)(4,1)}, bf16[8,16,2048]{2,1,0:T(8,128)(2,1)}...) while((s32[]{:T(128)}, f32[8,16,2048]{2,1,0:T(8,128)}, ...), condition=%wide.region_34.35_spmd.clone, body=%wide.region_27.34_spmd.clone.sunk | while | flops 272187520 | bytes 9770061 | solution.py:118
  141.4 7.8 %conditional.7 = (f32[1,16,2048]{2,1,0:T(8,128)S(1)}, f32[1,16,16]{1,2,0:T(8,128)}) conditional(s32[]{:T(128)} %bitcast.226, () %tuple.139, (pred[8]{0:T(512)(128)(4,1)S(1)}, s32[]{:T(128)}, bf16[2,4096,128]{2,1,0:T(8,128)(2,1)}, bf16[2,16,8,128]{3,2,0,1:T(8,128)(2,1)S(1)}, bf16[2,4096,128]{2,1,0:T(8,128)(2,1)S(1)}, /*index=5*/s32[8]{0:T(128)}, ...), branch_computations={%region_28.28_spmd, %region_29.33_spmd.clone} | conditional | flops 272187520 | bytes 9226141 | solution.py:116
  142.2 6.9 %while.59 = (s32[]{:T(128)}, f32[2,8,16,128]{3,2,1,0:T(8,128)S(1)}, f32[2,8,16]{2,1,0:T(8,128)}, s32[16]{0:T(128)S(1)}, bf16[2,4096,128]{2,1,0:T(8,128)(2,1)}, /...) while((s32[]{:T(128)}, f32[2,8,16,128]{3,2,1,0:T(8,128)S(1)}, ...), condition=%wide.region_33.32_spmd, body=%wide.region_30.31_spmd.sunk | while | flops 272187264 | bytes 8700569 | solution.py:99
  153.5 7.8 %conditional.7 = (f32[1,16,2048]{2,1,0:T(8,128)S(1)}, f32[1,16,16]{1,2,0:T(8,128)}) conditional(s32[]{:T(128)} %bitcast.226, () %tuple.139, (pred[8]{0:T(512)(128)(4,1)S(1)}, s32[]{:T(128)}, bf16[2,4096,128]{2,1,0:T(8,128)(2,1)}, bf16[2,16,8,128]{3,2,0,1:T(8,128)(2,1)S(1)}, bf16[2,4096,128]{2,1,0:T(8,128)(2,1)S(1)}, /*index=5*/s32[8]{0:T(128)}, ...), branch_computations={%region_28.28_spmd, %region_29.33_spmd.clone} | conditional | flops 272187520 | bytes 9226141 | solution.py:116
  154.3 6.9 %while.59 = (s32[]{:T(128)}, f32[2,8,16,128]{3,2,1,0:T(8,128)S(1)}, f32[2,8,16]{2,1,0:T(8,128)}, s32[16]{0:T(128)S(1)}, bf16[2,4096,128]{2,1,0:T(8,128)(2,1)}, /...) while((s32[]{:T(128)}, f32[2,8,16,128]{3,2,1,0:T(8,128)S(1)}, ...), condition=%wide.region_33.32_spmd, body=%wide.region_30.31_spmd.sunk | while | flops 272187264 | bytes 8700569 | solution.py:99
  193.3 46.6 %all-to-all-start.4 = ((f32[8,1,256]{2,1,0:T(1,128)}), f32[8,1,256]{2,1,0:T(1,128)S(1)}, u32[]{:S(2)}, u32[]{:S(2)}) async-start(f32[8,1,256]{2,1,0:T(1,128)} %reshape.622), calls=%async_computation.4 | async-start | bytes 16384 | tf_op jit(solution)/shard_map/all_to_all | solution.py:137
  246.5 3.6 %all-to-all-start.2 = ((f32[1,8,16,2048]{3,2,0,1:T(8,128)}), f32[1,8,16,2048]{3,2,0,1:T(8,128)S(1)}, u32[]{:S(2)}, u32[]{:S(2)}) async-start(f32[1,8,16,2048]{3,2,0,1:T(8,128)} %bitcast.42), calls=%async_computation.2 | async-start | bytes 2097152 | tf_op jit(solution)/shard_map/all_to_all | solution.py:130
  253.9 20.5 %all-to-all-done.2 = f32[1,8,16,2048]{3,2,0,1:T(8,128)S(1)} async-done(((f32[1,8,16,2048]{3,2,0,1:T(8,128)}), f32[1,8,16,2048]{3,2,0,1:T(8,128)S(1)}, u32[]{:S(2)}, u32[]{:S(2)}) %all-to-all-start.2) | async-done | bytes 1048608 | tf_op jit(solution)/shard_map/all_to_all | solution.py:130
  274.3 3.6 %all-to-all-start.5 = ((f32[1,8,16,2048]{3,2,0,1:T(8,128)}), f32[1,8,16,2048]{3,2,0,1:T(8,128)S(1)}, u32[]{:S(2)}, u32[]{:S(2)}) async-start(f32[1,8,16,2048]{3,2,0,1:T(8,128)} %bitcast.62), calls=%async_computation.5 | async-start | bytes 2097152 | tf_op jit(solution)/shard_map/all_to_all | solution.py:130
  286.2 17.4 %all-to-all-done.5 = f32[1,8,16,2048]{3,2,0,1:T(8,128)S(1)} async-done(((f32[1,8,16,2048]{3,2,0,1:T(8,128)}), f32[1,8,16,2048]{3,2,0,1:T(8,128)S(1)}, u32[]{:S(2)}, u32[]{:S(2)}) %all-to-all-start.5) | async-done | bytes 1048608 | tf_op jit(solution)/shard_map/all_to_all | solution.py:130
  (351 shorter events, 157.8 us)
Async XLA Ops:
  3.5 33.0 %all-to-all-start = ((bf16[1,8,16,2048]{3,2,0,1:T(8,128)(2,1)}), bf16[1,8,16,2048]{3,2,0,1:T(8,128)(2,1)S(1)}, u32[]{:S(2)}, u32[]{:S(2)}) async-start(bf16[1,8,16,2048]{3,2,0,1:T(8,128)(2,1)} %broadcast_select_fusion.1), calls=%async_computation | async-start | bytes 1048576 | tf_op jit(solution)/shard_map/all_to_all | solution.py:75
  10.9 5.3 %copy-start.1 = (pred[8]{0:T(512)(128)(4,1)}, pred[8]{0:T(512)(128)(4,1)S(1)}, u32[]{:S(2)}) copy-start(pred[8]{0:T(512)(128)(4,1)S(1)} %get-tuple-element.464) | copy-start | bytes 28
  13.2 2.9 copy-start.3
  36.6 69.0 %all-to-all-start.3 = ((bf16[1,8,16,2048]{3,2,0,1:T(8,128)(2,1)}), bf16[1,8,16,2048]{3,2,0,1:T(8,128)(2,1)}, u32[]{:S(2)}, u32[]{:S(2)}) async-start(bf16[1,8,16,2048]{3,2,0,1:T(8,128)(2,1)} %broadcast_select_fusion), calls=%async_computation.3 | async-start | bytes 1048576 | tf_op jit(solution)/shard_map/all_to_all | solution.py:75
  105.6 87.8 %all-to-all-start.1 = ((f32[8,1,256]{2,1,0:T(1,128)}), f32[8,1,256]{2,1,0:T(1,128)S(1)}, u32[]{:S(2)}, u32[]{:S(2)}) async-start(f32[8,1,256]{2,1,0:T(1,128)} %reshape.624), calls=%async_computation.1 | async-start | bytes 16384 | tf_op jit(solution)/shard_map/all_to_all | solution.py:137
  193.3 53.1 %all-to-all-start.4 = ((f32[8,1,256]{2,1,0:T(1,128)}), f32[8,1,256]{2,1,0:T(1,128)S(1)}, u32[]{:S(2)}, u32[]{:S(2)}) async-start(f32[8,1,256]{2,1,0:T(1,128)} %reshape.622), calls=%async_computation.4 | async-start | bytes 16384 | tf_op jit(solution)/shard_map/all_to_all | solution.py:137
  243.9 7.2 %copy-start = (f32[8,16,2048]{2,1,0:T(8,128)S(1)}, f32[8,16,2048]{2,1,0:T(8,128)}, u32[]{:S(2)}) copy-start(f32[8,16,2048]{2,1,0:T(8,128)} %get-tuple-element.234) | copy-start | bytes 3145732
  243.9 7.3 %copy-start.2 = (s32[8]{0:T(128)S(1)}, s32[8]{0:T(128)}, u32[]{:S(2)}) copy-start(s32[8]{0:T(128)} %get-tuple-element.546) | copy-start | bytes 100
  246.5 27.9 %all-to-all-start.2 = ((f32[1,8,16,2048]{3,2,0,1:T(8,128)}), f32[1,8,16,2048]{3,2,0,1:T(8,128)S(1)}, u32[]{:S(2)}, u32[]{:S(2)}) async-start(f32[1,8,16,2048]{3,2,0,1:T(8,128)} %bitcast.42), calls=%async_computation.2 | async-start | bytes 2097152 | tf_op jit(solution)/shard_map/all_to_all | solution.py:130
  251.2 26.8 %copy-start.5 = (s32[4]{0:T(128)S(1)}, s32[4]{0:T(128)}, u32[]{:S(2)}) copy-start(s32[4]{0:T(128)} %get-tuple-element.461) | copy-start | bytes 52
  251.2 26.8 %copy-start.4 = (s32[4]{0:T(128)S(1)}, s32[4]{0:T(128)}, u32[]{:S(2)}) copy-start(s32[4]{0:T(128)} %get-tuple-element.550) | copy-start | bytes 52
  274.3 29.2 %all-to-all-start.5 = ((f32[1,8,16,2048]{3,2,0,1:T(8,128)}), f32[1,8,16,2048]{3,2,0,1:T(8,128)S(1)}, u32[]{:S(2)}, u32[]{:S(2)}) async-start(f32[1,8,16,2048]{3,2,0,1:T(8,128)} %bitcast.62), calls=%async_computation.5 | async-start | bytes 2097152 | tf_op jit(solution)/shard_map/all_to_all | solution.py:130
where the time goes:
time: 310 us; the launch traced here: 305 us
  local copies, waits for them, and re-layouts  96.4 us (31%)
  starting transfers between devices  96.4 us (31%)
  waiting for transfers between devices  40.4 us (13%)
  other arithmetic  30.3 us (10%)
  matrix products  29.4 us (9%)
  loops' own time  11.6 us (4%)
    all_to_all x2, starting transfers between devices, local(): lax.all_to_all(out_mass.reshape(batch_here, seq_size, tile_rows, head_cou...  76 us
    all_to_all x2, waiting for transfers between devices, local(): lax.all_to_all(out_rows.reshape(batch_here, seq_size, tile_rows, features...  37.8 us
    dot_general x12, matrix products, attend(): jnp.einsum('rgh,kh->grk', tile_query, key_head, preferred_element_type=jn...  21 us
    dynamic_slice x16, local copies, waits for them, and re-layouts, local(): lax.map(one_slot, (arrived, horizons, slot_live))  20 us
    dynamic_update_slice x48, local copies, waits for them, and re-layouts, local(): lax.map(one_slot, (arrived, horizons, slot_live))  17.7 us
    unnamed x26, local copies, waits for them, and re-layouts  16.5 us
    while x32, local copies, waits for them, and re-layouts  13.7 us
    all_to_all x2, starting transfers between devices, local(): lax.all_to_all(outgoing, 'seq', split_axis=1, concat_axis=1, tiled=True)  13.3 us
  transfers between devices with their start and end apart: 6, of which 3 were waited for; matrix products, arithmetic and copies ran while one was open for 50% of the time, Pallas kernels for 0%

commit v1 on v0

v1 whole, which is shorter than its diff:
```python
import functools
import math

import jax
import jax.numpy as jnp
from jax import lax
from jax.experimental import pallas as pl
from jax.experimental.pallas import tpu as pltpu
from jax.sharding import PartitionSpec as P

HEAD = 128
CHUNK = 1024
MASKED = -1e30
RATE = HEAD ** (-0.5) * math.log2(math.e)
MESH = pl.DeviceIdType.MESH
F32 = jnp.float32
BF16 = jnp.bfloat16


def dot_t(a, b):
    return lax.dot_general(a, b, (((1,), (1,)), ((), ())), preferred_element_type=F32)


def kernel(
    n, block_ref, place_ref, offset_ref, q_hbm, k_hbm, v_hbm, out_ref,
    qbuf, kbuf, vbuf, masks, s0, s1, m0, m1, sbuf, rbuf, mass_s, mass_r, shares,
    kv_sem, q_local, q_send, q_recv, r_send, r_recv, c_send, c_recv,
):
    me = lax.axis_index("seq")
    batch, _, rows, features = q_hbm.shape
    block = k_hbm.shape[1]
    shared = k_hbm.shape[2] // HEAD
    group = features // k_hbm.shape[2]
    top = block_ref.shape[1]
    tile = group * rows
    total = batch * tile
    chunks = block // CHUNK
    scores = (s0, s1)
    peaks = (m0, m1)

    def distance(k):
        return k

    loads = []
    for c in range(shared):
        columns = pl.ds(c * HEAD, HEAD)
        loads.append((
            pltpu.make_async_copy(k_hbm.at[0, :, columns], kbuf.at[c], kv_sem.at[0, c]),
            pltpu.make_async_copy(v_hbm.at[0, :, columns], vbuf.at[c], kv_sem.at[1, c]),
        ))
    own_query = pltpu.make_async_copy(q_hbm.at[:, 0], qbuf.at[0], q_local.at[0])
    own_query.start()
    for c in range(shared):
        loads[c][0].start()
    for c in range(shared):
        loads[c][1].start()

    barrier = pltpu.get_barrier_semaphore()

    @pl.loop(1, n)
    def _(d):
        pl.semaphore_signal(barrier, inc=1, device_id={"seq": lax.rem(me + d, n)}, device_id_type=MESH)

    pl.semaphore_wait(barrier, n - 1)

    def query_copy(d):
        return pltpu.make_async_remote_copy(
            src_ref=q_hbm.at[:, 0], dst_ref=qbuf.at[n - d], send_sem=q_send.at[d], recv_sem=q_recv.at[n - d],
            device_id={"seq": lax.rem(me + d, n)}, device_id_type=MESH)

    def result_copy(d):
        return pltpu.make_async_remote_copy(
            src_ref=sbuf.at[d], dst_ref=rbuf.at[n - d], send_sem=r_send.at[d], recv_sem=r_recv.at[n - d],
            device_id={"seq": lax.rem(me + d, n)}, device_id_type=MESH)

    def mass_copy(d):
        return pltpu.make_async_remote_copy(
            src_ref=mass_s.at[d], dst_ref=mass_r.at[n - d], send_sem=c_send.at[d], recv_sem=c_recv.at[n - d],
            device_id={"seq": lax.rem(me + d, n)}, device_id_type=MESH)

    def query_arrival(d):
        return pltpu.make_async_remote_copy(
            src_ref=q_hbm.at[:, 0], dst_ref=qbuf.at[d], send_sem=q_send.at[d], recv_sem=q_recv.at[d],
            device_id={"seq": lax.rem(me + d, n)}, device_id_type=MESH)

    def result_arrival(d):
        return pltpu.make_async_remote_copy(
            src_ref=sbuf.at[d], dst_ref=rbuf.at[d], send_sem=r_send.at[d], recv_sem=r_recv.at[d],
            device_id={"seq": lax.rem(me + d, n)}, device_id_type=MESH)

    def mass_arrival(d):
        return pltpu.make_async_remote_copy(
            src_ref=mass_s.at[d], dst_ref=mass_r.at[d], send_sem=c_send.at[d], recv_sem=c_recv.at[d],
            device_id={"seq": lax.rem(me + d, n)}, device_id_type=MESH)

    @pl.loop(1, n)
    def _(k):
        query_copy(distance(k)).start()

    my_block = lax.fori_loop(
        0, place_ref.shape[0], lambda e, found: found + jnp.where(place_ref[e] == me, e, 0), jnp.int32(0))
    lanes = lax.broadcasted_iota(jnp.int32, (1, HEAD), 1)
    tile_lane = lax.broadcasted_iota(jnp.int32, (tile, HEAD), 1)
    tile_row = lax.rem(lax.broadcasted_iota(jnp.int32, (tile, HEAD), 0), rows)

    def first_hidden(d):
        hidden = jnp.zeros((1, HEAD), jnp.int32)
        for b in range(batch):
            t = b * n + lax.rem(me + d, n)
            entries = [block_ref[t, e] for e in range(top)]
            own = functools.reduce(jnp.maximum, entries)
            hits = functools.reduce(lambda x, y: x + y, [jnp.where(e == my_block, 1, 0) for e in entries])
            start = jnp.where(own == my_block, offset_ref[t] * rows, jnp.where(hits > 0, block, -2 * rows))
            column = lanes - b * rows
            hidden = jnp.where((column >= 0) & (column < rows), start + column + 1, hidden)
        return hidden

    def query_rows(d, c):
        parts = []
        for b in range(batch):
            piece = jnp.concatenate(
                [qbuf[d, b, :, pl.ds((c * group + g) * HEAD, HEAD)] for g in range(group)], axis=0)
            mark = jnp.where(tile_lane == tile_row + b * rows, MASKED, 0.0).astype(BF16)
            parts.append(jnp.concatenate([piece, mark], axis=1))
        return jnp.concatenate(parts, axis=0)

    def both(fresh, ready):
        if fresh is not None:
            d_new, c_new = fresh
            query = query_rows(d_new, c_new)
            peak = None
            if c_new == 0:
                hidden = first_hidden(d_new)
        if ready is not None:
            d_old, c_old = ready
            top_score = jnp.max(peaks[c_old][...], axis=1, keepdims=True)
            blend = jnp.zeros((total, 2 * HEAD), F32)
        for j in range(chunks):
            here = slice(j * CHUNK, (j + 1) * CHUNK)
            if fresh is not None:
                if c_new == 0:
                    position = lax.broadcasted_iota(jnp.int32, (CHUNK, HEAD), 0) + j * CHUNK
                    mask = jnp.where(position >= hidden, 1.0, 0.0).astype(BF16)
                    masks[here, :] = mask
                else:
                    mask = masks[here, :]
                part = dot_t(query, jnp.concatenate([kbuf[c_new, here, :], mask], axis=1))
                scores[c_new][:, here] = part
                for i in range(CHUNK // HEAD):
                    column = part[:, i * HEAD:(i + 1) * HEAD]
                    peak = column if peak is None else jnp.maximum(peak, column)
            if ready is not None:
                weights = jnp.exp2((scores[c_old][:, here] - top_score) * RATE).astype(BF16)
                value = jnp.concatenate([vbuf[c_old, here, :], jnp.ones((CHUNK, HEAD), BF16)], axis=1)
                blend = blend + jnp.dot(weights, value, preferred_element_type=F32)
        if fresh is not None:
            peaks[c_new][...] = peak
        if ready is not None:
            summed = blend[:, HEAD:]
            result = (blend[:, :HEAD] / summed).astype(BF16)
            mass = jnp.log2(summed) + top_score * RATE
            head_lane = lax.broadcasted_iota(jnp.int32, (rows, HEAD), 1)
            for b in range(batch):
                kept = jnp.zeros((rows, HEAD), F32) if c_old == 0 else mass_s[d_old, b]
                for g in range(group):
                    span = slice(b * tile + g * rows, b * tile + (g + 1) * rows)
                    head = c_old * group + g
                    sbuf[d_old, b, :, pl.ds(head * HEAD, HEAD)] = result[span]
                    kept = jnp.where(head_lane == head, mass[span], kept)
                mass_s[d_old, b] = kept

    own_query.wait()
    for c in range(shared):
        loads[c][0].wait()
        loads[c][1].wait()
    both((0, 0), None)

    def finish(d):
        result_copy(d).start()
        mass_copy(d).start()

    @pl.loop(0, n - 1)
    def _(k):
        d, later = distance(k), distance(k + 1)
        both((d, 1), (d, 0))
        query_arrival(later).wait_recv()
        both((later, 0), (d, 1))

        @pl.when(k > 0)
        def _():
            finish(d)

    last = distance(n - 1)
    both((last, 1), (last, 0))
    both(None, (last, 1))
    finish(last)

    @pl.loop(1, n)
    def _(d):
        mass_arrival(d).wait_recv()

    highest = mass_s[0]
    for_all = lambda f, init: lax.fori_loop(1, n, f, init)
    highest = for_all(lambda d, m: jnp.maximum(m, mass_r[d]), highest)
    bottom = for_all(lambda d, s: s + jnp.exp2(mass_r[d] - highest), jnp.exp2(mass_s[0] - highest))

    @pl.loop(1, n)
    def _(d):
        result_arrival(d).wait_recv()

    shares[0] = jnp.exp2(mass_s[0] - highest) / bottom

    @pl.loop(1, n)
    def _(d):
        shares[d] = jnp.exp2(mass_r[d] - highest) / bottom

    for b in range(batch):
        for head in range(shared * group):
            columns = pl.ds(head * HEAD, HEAD)

            def add(d, sofar):
                return sofar + shares[d, b][:, head:head + 1] * rbuf[d, b, :, columns].astype(F32)

            value = shares[0, b][:, head:head + 1] * sbuf[0, b, :, columns].astype(F32)
            out_ref[b, 0, :, columns] = lax.fori_loop(1, n, add, value, unroll=n <= 8).astype(BF16)

    @pl.loop(1, n)
    def _(d):
        query_copy(d).wait_send()
        result_copy(d).wait_send()
        mass_copy(d).wait_send()


def local(n, queries, keys, values, tile_blocks, block_place, tile_offset):
    batch, _, rows, features = queries.shape
    block = keys.shape[1]
    shared = keys.shape[2] // HEAD
    group = features // keys.shape[2]
    total = batch * group * rows
    smem = pl.BlockSpec(memory_space=pltpu.SMEM)
    far = pl.BlockSpec(memory_space=pl.ANY)
    dma = pltpu.SemaphoreType.DMA
    return pl.pallas_call(
        functools.partial(kernel, n),
        out_shape=jax.ShapeDtypeStruct(queries.shape, queries.dtype),
        in_specs=[smem, smem, smem, far, far, far],
        out_specs=pl.BlockSpec(memory_space=pltpu.VMEM),
        scratch_shapes=[
            pltpu.VMEM((n, batch, rows, features), BF16),
            pltpu.VMEM((shared, block, HEAD), BF16),
            pltpu.VMEM((shared, block, HEAD), BF16),
            pltpu.VMEM((block, HEAD), BF16),
            pltpu.VMEM((total, block), F32),
            pltpu.VMEM((total, block), F32),
            pltpu.VMEM((total, HEAD), F32),
            pltpu.VMEM((total, HEAD), F32),
            pltpu.VMEM((n, batch, rows, features), BF16),
            pltpu.VMEM((n, batch, rows, features), BF16),
            pltpu.VMEM((n, batch, rows, HEAD), F32),
            pltpu.VMEM((n, batch, rows, HEAD), F32),
            pltpu.VMEM((n, batch, rows, HEAD), F32),
            dma((2, shared)),
            dma((1,)),
            dma((n,)), dma((n,)), dma((n,)), dma((n,)), dma((n,)), dma((n,)),
        ],
        compiler_params=pltpu.CompilerParams(
            collective_id=0, has_side_effects=True, vmem_limit_bytes=60 * 1024 * 1024),
    )(tile_blocks, block_place, tile_offset, queries, keys, values)


def solution(mesh):
    placed = (
        P(None, ("groups", "seq"), None, "heads"),
        P(("groups", "seq"), None, "heads"),
        P(("groups", "seq"), None, "heads"),
        P("groups", None),
        P("groups"),
        P("groups"),
    )
    return jax.shard_map(
        functools.partial(local, mesh.shape["seq"]),
        mesh=mesh,
        in_specs=placed,
        out_specs=P(None, ("groups", "seq"), None, "heads"),
        check_vma=False,
    )
```

time: 310 us -> 69.3 us (0.22)
  the two profiles are of different devices: /device:TPU:0 before, /device:TPU:12 now
where the time goes in v1:
time: 69.3 us; the launch traced here: 69.1 us
  Pallas kernels  66.2 us (96%)
  local copies, waits for them, and re-layouts  2.92 us (4%)
    pallas_call x1, Pallas kernels, local(): pl.pallas_call(functools.partial(kernel, n), out_shape=jax.ShapeDtypeStru...  66.2 us
    unnamed x2, local copies, waits for them, and re-layouts  2.92 us

profile of v1, /device:TPU:12, one launch (start us, length us, event | category | flops | bytes accessed | tf_op | source)
XLA Modules:
  0.0 69.1 jit_solution(9611440287416600641)
XLA Ops:
  0.0 1.4 %copy.7.block_ref = s32[16,4]{1,0:T(8,128)} copy(s32[16,4]{0,1:T(4,128)} %param.9) | data formatting | bytes 512 | tf_op args[3]
  1.4 66.2 %shard_map.64 = bf16[2,1,16,2048]{3,2,1,0:T(8,128)(2,1)} custom-call(s32[16,4]{1,0:T(8,128)} %copy.7.block_ref, s32[8]{0:T(128)} %place_ref.1, s32[16]{0:T(128)} %offset_ref.1, bf16[2,1,16,2048]{3,2,1,0:T(8,128)(2,1)} %q_hbm.1, bf16[1,4096,256]{2,1,0:T(8,128)(2,1)} %k_hbm.1, bf16[1,4096,256]{2,1,0:T(8,128)(2,1)} %v_hbm.1), custom_call_target="tpu_custom_call" | custom-call | tf_op jit(solution)/shard_map/pallas_call | solution.py:243
  67.6 1.6 %copy.9 = bf16[2,1,16,2048]{3,2,1,0:T(8,128)(2,1)} copy(bf16[2,1,16,2048]{3,2,1,0:T(8,128)(2,1)} %shard_map.64) | data formatting | bytes 262144

commit v2 on v1

--- a/solution.py
+++ b/solution.py
@@ -23,8 +23,8 @@
 
 def kernel(
     n, block_ref, place_ref, offset_ref, q_hbm, k_hbm, v_hbm, out_ref,
-    qbuf, kbuf, vbuf, masks, s0, s1, m0, m1, sbuf, rbuf, mass_s, mass_r, shares,
-    kv_sem, q_local, q_send, q_recv, r_send, r_recv, c_send, c_recv,
+    qbuf, kbuf, vbuf, masks, s0, s1, m0, m1, sbuf, mass_s, xbuf, mass_x, gbuf, mass_g, rbuf, mass_r, shares,
+    kv_sem, q_local, q_send, q_recv, f_send, f_recv, x_send, x_recv, y_send, y_recv, r_send, r_recv, c_send, c_recv,
 ):
     me = lax.axis_index("seq")
     batch, _, rows, features = q_hbm.shape
@@ -38,8 +38,11 @@
     scores = (s0, s1)
     peaks = (m0, m1)
 
-    def distance(k):
-        return k
+    lines = n // 2
+    line, side = me // 2, lax.rem(me, 2)
+
+    def device(j, p):
+        return lax.rem(line + j, lines) * 2 + lax.rem(side + p, 2)
 
     loads = []
     for c in range(shared):
@@ -57,45 +60,42 @@
 
     barrier = pltpu.get_barrier_semaphore()
 
-    @pl.loop(1, n)
-    def _(d):
-        pl.semaphore_signal(barrier, inc=1, device_id={"seq": lax.rem(me + d, n)}, device_id_type=MESH)
-
-    pl.semaphore_wait(barrier, n - 1)
-
-    def query_copy(d):
+    def greet(target):
+        pl.semaphore_signal(barrier, inc=1, device_id={"seq": target}, device_id_type=MESH)
+
+    greet(device(0, 1))
+
+    @pl.loop(1, lines)
+    def _(j):
+        greet(device(j, 0))
+
+    pl.semaphore_wait(barrier, lines)
+
+    def remote(src, dst, send, recv, target):
         return pltpu.make_async_remote_copy(
-            src_ref=q_hbm.at[:, 0], dst_ref=qbuf.at[n - d], send_sem=q_send.at[d], recv_sem=q_recv.at[n - d],
-            device_id={"seq": lax.rem(me + d, n)}, device_id_type=MESH)
-
-    def result_copy(d):
-        return pltpu.make_async_remote_copy(
-            src_ref=sbuf.at[d], dst_ref=rbuf.at[n - d], send_sem=r_send.at[d], recv_sem=r_recv.at[n - d],
-            device_id={"seq": lax.rem(me + d, n)}, device_id_type=MESH)
-
-    def mass_copy(d):
-        return pltpu.make_async_remote_copy(
-            src_ref=mass_s.at[d], dst_ref=mass_r.at[n - d], send_sem=c_send.at[d], recv_sem=c_recv.at[n - d],
-            device_id={"seq": lax.rem(me + d, n)}, device_id_type=MESH)
-
-    def query_arrival(d):
-        return pltpu.make_async_remote_copy(
-            src_ref=q_hbm.at[:, 0], dst_ref=qbuf.at[d], send_sem=q_send.at[d], recv_sem=q_recv.at[d],
-            device_id={"seq": lax.rem(me + d, n)}, device_id_type=MESH)
-
-    def result_arrival(d):
-        return pltpu.make_async_remote_copy(
-            src_ref=sbuf.at[d], dst_ref=rbuf.at[d], send_sem=r_send.at[d], recv_sem=r_recv.at[d],
-            device_id={"seq": lax.rem(me + d, n)}, device_id_type=MESH)
-
-    def mass_arrival(d):
-        return pltpu.make_async_remote_copy(
-            src_ref=mass_s.at[d], dst_ref=mass_r.at[d], send_sem=c_send.at[d], recv_sem=c_recv.at[d],
-            device_id={"seq": lax.rem(me + d, n)}, device_id_type=MESH)
-
-    @pl.loop(1, n)
-    def _(k):
-        query_copy(distance(k)).start()
+            src_ref=src, dst_ref=dst, send_sem=send, recv_sem=recv,
+            device_id={"seq": target}, device_id_type=MESH)
+
+    def query_copy(j, there):
+        return remote(q_hbm.at[:, 0], qbuf.at[2 * there], q_send.at[j], q_recv.at[there], device(j, 0))
+
+    def forward_copy(j):
+        return remote(qbuf.at[2 * j], qbuf.at[2 * j + 1], f_send.at[j], f_recv.at[j], device(0, 1))
+
+    def cross_copies(j):
+        return (remote(sbuf.at[2 * j + 1], xbuf.at[j], x_send.at[j], x_recv.at[j], device(0, 1)),
+                remote(mass_s.at[2 * j + 1], mass_x.at[j], y_send.at[j], y_recv.at[j], device(0, 1)))
+
+    def return_copies(j, there):
+        return (remote(gbuf.at[j], rbuf.at[there], r_send.at[j], r_recv.at[there], device(j, 0)),
+                remote(mass_g.at[j], mass_r.at[there], c_send.at[j], c_recv.at[there], device(j, 0)))
+
+    @pl.loop(1, lines)
+    def _(j):
+        query_copy(j, lines - j).start()
+
+    own_query.wait()
+    forward_copy(0).start()
 
     my_block = lax.fori_loop(
         0, place_ref.shape[0], lambda e, found: found + jnp.where(place_ref[e] == me, e, 0), jnp.int32(0))
@@ -106,7 +106,7 @@
     def first_hidden(d):
         hidden = jnp.zeros((1, HEAD), jnp.int32)
         for b in range(batch):
-            t = b * n + lax.rem(me + d, n)
+            t = b * n + device(d // 2, lax.rem(d, 2))
             entries = [block_ref[t, e] for e in range(top)]
             own = functools.reduce(jnp.maximum, entries)
             hits = functools.reduce(lambda x, y: x + y, [jnp.where(e == my_block, 1, 0) for e in entries])
@@ -169,66 +169,96 @@
                     kept = jnp.where(head_lane == head, mass[span], kept)
                 mass_s[d_old, b] = kept
 
-    own_query.wait()
     for c in range(shared):
         loads[c][0].wait()
         loads[c][1].wait()
     both((0, 0), None)
 
-    def finish(d):
-        result_copy(d).start()
-        mass_copy(d).start()
-
-    @pl.loop(0, n - 1)
-    def _(k):
-        d, later = distance(k), distance(k + 1)
-        both((d, 1), (d, 0))
-        query_arrival(later).wait_recv()
-        both((later, 0), (d, 1))
-
-        @pl.when(k > 0)
+    def merge(j):
+        for copy in cross_copies(j):
+            copy.wait_recv()
+        for b in range(batch):
+            mine, other = mass_s[2 * j, b], mass_x[j, b]
+            highest = jnp.maximum(mine, other)
+            first, second = jnp.exp2(mine - highest), jnp.exp2(other - highest)
+            bottom = first + second
+            mass_g[j, b] = highest + jnp.log2(bottom)
+            first, second = first / bottom, second / bottom
+            for head in range(shared * group):
+                columns = pl.ds(head * HEAD, HEAD)
+                gbuf[j, b, :, columns] = (
+                    first[:, head:head + 1] * sbuf[2 * j, b, :, columns].astype(F32)
+                    + second[:, head:head + 1] * xbuf[j, b, :, columns].astype(F32)).astype(BF16)
+
+    def finish(j):
+        merge(j)
+
+        @pl.when(j > 0)
         def _():
-            finish(d)
-
-    last = distance(n - 1)
-    both((last, 1), (last, 0))
-    both(None, (last, 1))
-    finish(last)
-
-    @pl.loop(1, n)
-    def _(d):
-        mass_arrival(d).wait_recv()
-
-    highest = mass_s[0]
-    for_all = lambda f, init: lax.fori_loop(1, n, f, init)
-    highest = for_all(lambda d, m: jnp.maximum(m, mass_r[d]), highest)
-    bottom = for_all(lambda d, s: s + jnp.exp2(mass_r[d] - highest), jnp.exp2(mass_s[0] - highest))
-
-    @pl.loop(1, n)
-    def _(d):
-        result_arrival(d).wait_recv()
-
-    shares[0] = jnp.exp2(mass_s[0] - highest) / bottom
-
-    @pl.loop(1, n)
-    def _(d):
-        shares[d] = jnp.exp2(mass_r[d] - highest) / bottom
+            for copy in return_copies(j, lines - j):
+                copy.start()
+
+    def step(j, more):
+        near, far = 2 * j, 2 * j + 1
+        both((near, 1), (near, 0))
+        forward_copy(j).wait_recv()
+        both((far, 0), (near, 1))
+        if more:
+            query_copy(j + 1, j + 1).wait_recv()
+            forward_copy(j + 1).start()
+        both((far, 1), (far, 0))
+        both((2 * j + 2, 0) if more else None, (far, 1))
+        for copy in cross_copies(j):
+            copy.start()
+
+    @pl.loop(0, lines - 1)
+    def _(j):
+        step(j, True)
+
+        @pl.when(j > 0)
+        def _():
+            finish(j - 1)
+
+    step(lines - 1, False)
+    if lines > 1:
+        finish(lines - 2)
+    finish(lines - 1)
+
+    @pl.loop(1, lines)
+    def _(j):
+        for copy in return_copies(j, j):
+            copy.wait_recv()
+
+    for_all = lambda f, init: lax.fori_loop(1, lines, f, init)
+    highest = for_all(lambda j, m: jnp.maximum(m, mass_r[j]), mass_g[0])
+    bottom = for_all(lambda j, total_: total_ + jnp.exp2(mass_r[j] - highest), jnp.exp2(mass_g[0] - highest))
+    shares[0] = jnp.exp2(mass_g[0] - highest) / bottom
+
+    @pl.loop(1, lines)
+    def _(j):
+        shares[j] = jnp.exp2(mass_r[j] - highest) / bottom
 
     for b in range(batch):
         for head in range(shared * group):
             columns = pl.ds(head * HEAD, HEAD)
 
-            def add(d, sofar):
-                return sofar + shares[d, b][:, head:head + 1] * rbuf[d, b, :, columns].astype(F32)
-
-            value = shares[0, b][:, head:head + 1] * sbuf[0, b, :, columns].astype(F32)
-            out_ref[b, 0, :, columns] = lax.fori_loop(1, n, add, value, unroll=n <= 8).astype(BF16)
-
-    @pl.loop(1, n)
-    def _(d):
-        query_copy(d).wait_send()
-        result_copy(d).wait_send()
-        mass_copy(d).wait_send()
+            def add(j, sofar):
+                return sofar + shares[j, b][:, head:head + 1] * rbuf[j, b, :, columns].astype(F32)
+
+            value = shares[0, b][:, head:head + 1] * gbuf[0, b, :, columns].astype(F32)
+            out_ref[b, 0, :, columns] = lax.fori_loop(1, lines, add, value, unroll=n <= 8).astype(BF16)
+
+    @pl.loop(0, lines)
+    def _(j):
+        forward_copy(j).wait_send()
+        for copy in cross_copies(j):
+            copy.wait_send()
+
+    @pl.loop(1, lines)
+    def _(j):
+        query_copy(j, j).wait_send()
+        for copy in return_copies(j, j):
+            copy.wait_send()
 
 
 def local(n, queries, keys, values, tile_blocks, block_place, tile_offset):
@@ -237,6 +267,7 @@
     shared = keys.shape[2] // HEAD
     group = features // keys.shape[2]
     total = batch * group * rows
+    lines = n // 2
     smem = pl.BlockSpec(memory_space=pltpu.SMEM)
     far = pl.BlockSpec(memory_space=pl.ANY)
     dma = pltpu.SemaphoreType.DMA
@@ -255,13 +286,17 @@
             pltpu.VMEM((total, HEAD), F32),
             pltpu.VMEM((total, HEAD), F32),
             pltpu.VMEM((n, batch, rows, features), BF16),
-            pltpu.VMEM((n, batch, rows, features), BF16),
             pltpu.VMEM((n, batch, rows, HEAD), F32),
-            pltpu.VMEM((n, batch, rows, HEAD), F32),
-            pltpu.VMEM((n, batch, rows, HEAD), F32),
+            pltpu.VMEM((lines, batch, rows, features), BF16),
+            pltpu.VMEM((lines, batch, rows, HEAD), F32),
+            pltpu.VMEM((lines, batch, rows, features), BF16),
+            pltpu.VMEM((lines, batch, rows, HEAD), F32),
+            pltpu.VMEM((lines, batch, rows, features), BF16),
+            pltpu.VMEM((lines, batch, rows, HEAD), F32),
+            pltpu.VMEM((lines, batch, rows, HEAD), F32),
             dma((2, shared)),
             dma((1,)),
-            dma((n,)), dma((n,)), dma((n,)), dma((n,)), dma((n,)), dma((n,)),
+            *[dma((lines,))] * 12,
         ],
         compiler_params=pltpu.CompilerParams(
             collective_id=0, has_side_effects=True, vmem_limit_bytes=60 * 1024 * 1024),

time: 69.3 us -> 52.1 us (0.75)
  the two profiles are of different devices: /device:TPU:12 before, /device:TPU:0 now
where the time goes in v2:
time: 52.1 us; the launch traced here: 51.9 us
  Pallas kernels  49 us (94%)
  local copies, waits for them, and re-layouts  2.92 us (6%)
    pallas_call x1, Pallas kernels, local(): pl.pallas_call(functools.partial(kernel, n), out_shape=jax.ShapeDtypeStru...  49 us
    unnamed x2, local copies, waits for them, and re-layouts  2.92 us

profile of v2, /device:TPU:0, one launch (start us, length us, event | category | flops | bytes accessed | tf_op | source)
XLA Modules:
  0.0 51.9 jit_solution(18127636631087584721)
XLA Ops:
  0.0 1.4 %copy.7.block_ref = s32[16,4]{1,0:T(8,128)} copy(s32[16,4]{0,1:T(4,128)} %param.9) | data formatting | bytes 512 | tf_op args[3]
  1.4 49.0 %shard_map.64 = bf16[2,1,16,2048]{3,2,1,0:T(8,128)(2,1)} custom-call(s32[16,4]{1,0:T(8,128)} %copy.7.block_ref, s32[8]{0:T(128)} %place_ref.1, s32[16]{0:T(128)} %offset_ref.1, bf16[2,1,16,2048]{3,2,1,0:T(8,128)(2,1)} %q_hbm.1, bf16[1,4096,256]{2,1,0:T(8,128)(2,1)} %k_hbm.1, bf16[1,4096,256]{2,1,0:T(8,128)(2,1)} %v_hbm.1), custom_call_target="tpu_custom_call" | custom-call | tf_op jit(solution)/shard_map/pallas_call | solution.py:274
  50.3 1.6 %copy.9 = bf16[2,1,16,2048]{3,2,1,0:T(8,128)(2,1)} copy(bf16[2,1,16,2048]{3,2,1,0:T(8,128)(2,1)} %shard_map.64) | data formatting | bytes 262144

commit v3 on v2

--- a/solution.py
+++ b/solution.py
@@ -207,6 +207,12 @@
             query_copy(j + 1, j + 1).wait_recv()
             forward_copy(j + 1).start()
         both((far, 1), (far, 0))
+        if more:
+            @pl.when(j > 0)
+            def _():
+                finish(j - 1)
+        elif lines > 1:
+            finish(j - 1)
         both((2 * j + 2, 0) if more else None, (far, 1))
         for copy in cross_copies(j):
             copy.start()
@@ -215,13 +221,7 @@
     def _(j):
         step(j, True)
 
-        @pl.when(j > 0)
-        def _():
-            finish(j - 1)
-
     step(lines - 1, False)
-    if lines > 1:
-        finish(lines - 2)
     finish(lines - 1)
 
     @pl.loop(1, lines)

time: 52.1 us -> 54 us (1.036)
  Pallas kernels: 49 us -> 50.9 us
    pallas_call x1, Pallas kernels: 49 us -> 50.9 us  [local(): pl.pallas_call(functools.partial(kernel, n), out_shape=jax.ShapeDtypeStru...]
where the time goes in v3:
time: 54 us; the launch traced here: 53.8 us
  Pallas kernels  50.9 us (94%)
  local copies, waits for them, and re-layouts  2.92 us (5%)
    pallas_call x1, Pallas kernels, local(): pl.pallas_call(functools.partial(kernel, n), out_shape=jax.ShapeDtypeStru...  50.9 us
    unnamed x2, local copies, waits for them, and re-layouts  2.92 us

profile of v3, /device:TPU:0, one launch (start us, length us, event | category | flops | bytes accessed | tf_op | source)
XLA Modules:
  0.0 53.8 jit_solution(12014296281672380636)
XLA Ops:
  0.0 1.4 %copy.7.block_ref = s32[16,4]{1,0:T(8,128)} copy(s32[16,4]{0,1:T(4,128)} %param.9) | data formatting | bytes 512 | tf_op args[3]
  1.4 50.9 %shard_map.64 = bf16[2,1,16,2048]{3,2,1,0:T(8,128)(2,1)} custom-call(s32[16,4]{1,0:T(8,128)} %copy.7.block_ref, s32[8]{0:T(128)} %place_ref.1, s32[16]{0:T(128)} %offset_ref.1, bf16[2,1,16,2048]{3,2,1,0:T(8,128)(2,1)} %q_hbm.1, bf16[1,4096,256]{2,1,0:T(8,128)(2,1)} %k_hbm.1, bf16[1,4096,256]{2,1,0:T(8,128)(2,1)} %v_hbm.1), custom_call_target="tpu_custom_call" | custom-call | tf_op jit(solution)/shard_map/pallas_call | solution.py:274
  52.3 1.6 %copy.9 = bf16[2,1,16,2048]{3,2,1,0:T(8,128)(2,1)} copy(bf16[2,1,16,2048]{3,2,1,0:T(8,128)(2,1)} %shard_map.64) | data formatting | bytes 262144
